TPU v7x, 32 devices: a whole 2x2x4 slice. The times are simulated.
32 devices in a mesh: scan: 8 (over z, x), bin: 4 (over y, core).
Axes of the slice: x: 2, y: 2, z: 4, core: 2. Of those that a mesh axis runs over, the one named last changes fastest.
Arguments:
- tile_blocks: bfloat16 [64, 16, 256, 256], P('scan', 'bin'), may hold values from -0.25 to 0.25
- tile_pattern: int32 [2, 64], P(None, 'scan'), may hold values from 0 to 63, as said below
- tile_count: int32 [8], P('scan'), may hold values from 1 to 8, as said below
- initial_map: float32 [16, 4, 4096], P('bin', None, 'scan')
- measured: float32 [16, 4, 16384], P('bin', None, 'scan')
- step_size: float32 [1], replicated, may hold values from 0.06 to 0.1
- penalty: float32 [4096], P('scan'), may hold values from 40 to 200
Outputs:
- source_map: float32 [16, 4, 4096], P('bin', None, 'scan')
Inputs may be any that keep to these rules, and one draw needn't show every extreme that they name: `tile_pattern`: row 0 names a sensor block of 64; row 1 of slot s names one of the 2 scan tiles (s // 8) * 2 to (s // 8) * 2 + 1. Only the first tile_count[d] slots of index d of scan are live; in every draw some indices have all 8 slots live.
All inputs are finite; a program needn't handle non-finite values.
Results may differ from a plain program's by a relative error of at most 0.00074.
Values may be sent and summed in bfloat16 or wider, within the bound.
No kernel may reach another device: no remote copies, remote signals or barrier semaphores. Data moves between devices by JAX's collectives and lax.ppermute only.
A program may use at most 64 MiB of HBM per device.

v0:
```python
import jax
import jax.numpy as jnp
from jax import lax
from jax.sharding import PartitionSpec as P

ITERS = 2


def add_forward(partial_value, tile_set, block_rows, block_cols, points, first_slot, end_slot):
    tile_width = tile_set.shape[-1]

    def advance(slot_id, running):
        matrix = lax.dynamic_index_in_dim(tile_set, slot_id, 0, keepdims=False)
        source = lax.dynamic_slice_in_dim(points, block_cols[slot_id] * tile_width, tile_width, 2)
        contrib = jnp.einsum("fij,fsj->fsi", matrix, source, preferred_element_type=jnp.float32)
        start = block_rows[slot_id] * tile_width
        present = lax.dynamic_slice_in_dim(running, start, tile_width, 2)
        return lax.dynamic_update_slice_in_dim(running, present + contrib, start, 2)

    return lax.fori_loop(first_slot, end_slot, advance, partial_value)


def add_backward(gradient, tile_set, block_rows, block_cols, residual, first_slot, end_slot):
    tile_width = tile_set.shape[-1]

    def advance(slot_id, running):
        matrix = lax.dynamic_index_in_dim(tile_set, slot_id, 0, keepdims=False)
        source = lax.dynamic_slice_in_dim(residual, block_rows[slot_id] * tile_width, tile_width, 2)
        contrib = jnp.einsum("fij,fsi->fsj", matrix, source, preferred_element_type=jnp.float32)
        start = block_cols[slot_id] * tile_width
        present = lax.dynamic_slice_in_dim(running, start, tile_width, 2)
        return lax.dynamic_update_slice_in_dim(running, present + contrib, start, 2)

    return lax.fori_loop(first_slot, end_slot, advance, gradient)


def home_slots(rows, tile_width, sensors_dev, homed):
    return rows * tile_width // sensors_dev * homed + rows % homed


def body(tile_blocks, tile_pattern, tile_count, initial_map, measured, step_size, penalty):
    tile_width = tile_blocks.shape[-1]
    per_device = initial_map.shape[2] // tile_width
    block_rows = tile_pattern[0]
    block_cols = tile_pattern[1] - lax.axis_index("scan") * per_device
    live_count = tile_count[0]
    bins_dev, snapshots, sensors_dev = measured.shape
    scan_count = lax.axis_size("scan")
    sensors = sensors_dev * scan_count
    homed = max(1, sensors_dev // tile_width)
    measured_all = lax.all_gather(measured, "scan", axis=2, tiled=True)
    block_rows = home_slots(block_rows, tile_width, sensors_dev, homed)
    own_measured = lax.dynamic_slice_in_dim(
        measured_all, lax.axis_index("scan") * sensors_dev, homed * tile_width, 2
    )
    sensors = scan_count * homed * tile_width
    current = initial_map
    for iteration in range(ITERS):
        rounded_map = current.astype(jnp.bfloat16)
        partial_value = jnp.zeros((bins_dev, snapshots, sensors), jnp.float32)
        partial_value = add_forward(
            partial_value, tile_blocks, block_rows, block_cols, rounded_map, 0, live_count
        )
        outgoing = partial_value.reshape(bins_dev, snapshots, scan_count, homed * tile_width)
        arrived = lax.all_to_all(outgoing, "scan", split_axis=2, concat_axis=2, tiled=True)
        totals = jnp.sum(arrived, axis=2)
        rounded = (totals - own_measured).astype(jnp.bfloat16)
        residual = lax.all_gather(rounded, "scan", axis=2, tiled=True)
        gradient = jnp.zeros_like(current)
        gradient = add_backward(
            gradient, tile_blocks, block_rows, block_cols, residual, 0, live_count
        )
        moved = current - step_size[0] * gradient
        energy = lax.psum(jnp.sum(moved * moved, axis=(0, 1)), "bin")
        current = moved * jnp.maximum(0.0, 1.0 - step_size[0] * penalty / jnp.sqrt(energy + 1e-06))
    return current


def solution(mesh):
    in_specs = (
        P("scan", "bin", None, None),
        P(None, "scan"),
        P("scan"),
        P("bin", None, "scan"),
        P("bin", None, "scan"),
        P(),
        P("scan"),
    )
    out_specs = P("bin", None, "scan")
    return jax.shard_map(body, mesh=mesh, in_specs=in_specs, out_specs=out_specs, check_vma=False)
```

profile of v0, /device:TPU:12, one launch (start us, length us, event | category | flops | bytes accessed | tf_op | source)
XLA Modules:
  0.0 327.0 jit_solution(14422891736312756115)
XLA Ops:
  8.8 38.3 %while.40 = (s32[]{:T(128)}, f32[4,4,16384]{2,1,0:T(4,128)S(1)}, s32[]{:T(128)}, s32[8]{0:T(128)S(1)}, s32[8]{0:T(128)S(1)}, /*index=5*/bf16[4,4,512]{2,1,0:T(4,...) while((s32[]{:T(128)}, f32[4,4,16384]{2,1,0:T(4,128)S(1)}, ...), condition=%wide.region_1.2_spmd, body=%wide.region_0.1_spmd.sunk | while | flops 2101261 | bytes 565535 | solution.py:20
  12.2 1.3 fusion.36
  16.9 1.3 fusion.36
  21.6 1.3 fusion.36
  26.4 1.3 fusion.36
  31.1 1.3 fusion.36
  35.8 1.3 fusion.36
  40.5 1.3 fusion.36
  45.2 1.3 fusion.36
  47.2 1.1 copy.15
  48.3 5.5 %all-to-all-start = ((f32[4,4,8,2048]{3,1,0,2:T(4,128)}), f32[4,4,8,2048]{3,1,0,2:T(4,128)S(1)}, u32[]{:S(2)}, u32[]{:S(2)}) async-start(f32[4,4,8,2048]{3,1,0,2:T(4,128)} %bitcast.36), calls=%async_computation | async-start | bytes 2097152 | tf_op jit(solution)/shard_map/all_to_all | solution.py:65
  55.1 26.2 %all-to-all-done = f32[4,4,8,2048]{3,1,0,2:T(4,128)S(1)} async-done(((f32[4,4,8,2048]{3,1,0,2:T(4,128)}), f32[4,4,8,2048]{3,1,0,2:T(4,128)S(1)}, u32[]{:S(2)}, u32[]{:S(2)}) %all-to-all-start) | async-done | bytes 1048608 | tf_op jit(solution)/shard_map/all_to_all | solution.py:65
  81.5 20.1 %all-gather.2.cloned.1.call-done = f32[4,4,16384]{2,1,0:T(4,128)} async-done(((f32[4,4,2048]{2,1,0:T(4,128)}), f32[4,4,16384]{2,1,0:T(4,128)}) %all-gather.2.cloned.1.call-update) | async-done | bytes 1048592 | tf_op jit(solution)/shard_map/all_gather | solution.py:51
  102.6 29.9 %all_gather.10 = bf16[4,4,16384]{2,1,0:T(4,128)(2,1)S(1)} all-gather(bf16[4,4,2048]{2,1,0:T(4,128)(2,1)S(1)} %subtract_convert_fusion.1), channel_id=1, replica_groups=mesh['scan'=8,'bin'=4] {'scan'}, dimensions={2}, use_global_device_ids=true | all-gather | bytes 589824 | tf_op jit(solution)/shard_map/all_gather | solution.py:68
  132.5 37.8 %while.41 = (s32[]{:T(128)}, f32[4,4,512]{2,1,0:T(4,128)S(1)}, s32[]{:T(128)}, s32[8]{0:T(128)S(1)}, s32[8]{0:T(128)S(1)}, /*index=5*/bf16[4,4,16384]{2,1,0:T(4,...) while((s32[]{:T(128)}, f32[4,4,512]{2,1,0:T(4,128)S(1)}, ...), condition=%wide.region_4.5_spmd, body=%wide.region_3.4_spmd.sunk | while | flops 2101261 | bytes 565535 | solution.py:34
  135.9 1.2 fusion.39
  140.5 1.2 fusion.39
  145.2 1.2 fusion.39
  149.8 1.2 fusion.39
  154.5 1.2 fusion.39
  159.1 1.2 fusion.39
  163.7 1.2 fusion.39
  168.4 1.2 fusion.39
  170.3 5.9 %psum.14 = f32[512]{0:T(512)S(1)} all-reduce(f32[512]{0:T(512)S(1)} %get-tuple-element.217), channel_id=1, replica_groups=mesh['scan'=8,'bin'=4] {'bin'}, use_global_device_ids=true, to_apply=%region_6.7 | all-reduce | flops 512 | bytes 4096 | tf_op jit(solution)/shard_map/psum | solution.py:74
  176.4 38.3 %while.42 = (s32[]{:T(128)}, f32[4,4,16384]{2,1,0:T(4,128)S(1)}, s32[]{:T(128)}, s32[8]{0:T(128)S(1)}, s32[8]{0:T(128)S(1)}, /*index=5*/bf16[4,4,512]{2,1,0:T(4,...) while((s32[]{:T(128)}, f32[4,4,16384]{2,1,0:T(4,128)S(1)}, ...), condition=%wide.region_8.9_spmd, body=%wide.region_7.8_spmd.sunk | while | flops 2101261 | bytes 565535 | solution.py:20
  179.8 1.3 fusion.42
  184.5 1.3 fusion.42
  189.2 1.3 fusion.42
  193.9 1.3 fusion.42
  198.6 1.3 fusion.42
  203.3 1.3 fusion.42
  208.0 1.3 fusion.42
  212.7 1.3 fusion.42
  214.7 1.1 copy.14
  215.8 5.1 %all-to-all-start.1 = ((f32[4,4,8,2048]{3,1,0,2:T(4,128)}), f32[4,4,8,2048]{3,1,0,2:T(4,128)S(1)}, u32[]{:S(2)}, u32[]{:S(2)}) async-start(f32[4,4,8,2048]{3,1,0,2:T(4,128)} %bitcast.35), calls=%async_computation.1 | async-start | bytes 2097152 | tf_op jit(solution)/shard_map/all_to_all | solution.py:65
  220.9 23.2 %all-to-all-done.1 = f32[4,4,8,2048]{3,1,0,2:T(4,128)S(1)} async-done(((f32[4,4,8,2048]{3,1,0,2:T(4,128)}), f32[4,4,8,2048]{3,1,0,2:T(4,128)S(1)}, u32[]{:S(2)}, u32[]{:S(2)}) %all-to-all-start.1) | async-done | bytes 1048608 | tf_op jit(solution)/shard_map/all_to_all | solution.py:65
  244.3 0.9 subtract_convert_fusion
  245.2 30.7 %all_gather.11 = bf16[4,4,16384]{2,1,0:T(4,128)(2,1)S(1)} all-gather(bf16[4,4,2048]{2,1,0:T(4,128)(2,1)S(1)} %subtract_convert_fusion), channel_id=1, replica_groups=mesh['scan'=8,'bin'=4] {'scan'}, dimensions={2}, use_global_device_ids=true | all-gather | bytes 589824 | tf_op jit(solution)/shard_map/all_gather | solution.py:68
  275.9 37.8 %while.43 = (s32[]{:T(128)}, f32[4,4,512]{2,1,0:T(4,128)S(1)}, s32[]{:T(128)}, s32[8]{0:T(128)S(1)}, s32[8]{0:T(128)S(1)}, /*index=5*/bf16[4,4,16384]{2,1,0:T(4,...) while((s32[]{:T(128)}, f32[4,4,512]{2,1,0:T(4,128)S(1)}, ...), condition=%wide.region_11.12_spmd, body=%wide.region_10.11_spmd.sunk | while | flops 2101261 | bytes 565535 | solution.py:34
  279.4 1.2 fusion.45
  284.0 1.2 fusion.45
  288.6 1.2 fusion.45
  293.3 1.2 fusion.45
  297.9 1.2 fusion.45
  302.6 1.2 fusion.45
  307.2 1.2 fusion.45
  311.9 1.2 fusion.45
  313.8 5.8 %psum.15 = f32[512]{0:T(512)S(1)} all-reduce(f32[512]{0:T(512)S(1)} %multiply_reduce_fusion), channel_id=1, replica_groups=mesh['scan'=8,'bin'=4] {'bin'}, use_global_device_ids=true, to_apply=%region_13.14 | all-reduce | flops 512 | bytes 4096 | tf_op jit(solution)/shard_map/psum | solution.py:74
  (86 shorter events, 47.9 us)
Async XLA Ops:
  48.3 122.0 %copy-start = (f32[4,4,512]{2,1,0:T(4,128)S(1)}, f32[4,4,512]{2,1,0:T(4,128)}, u32[]{:S(2)}) copy-start(f32[4,4,512]{2,1,0:T(4,128)} %param.18) | copy-start | bytes 98308
  48.3 127.9 %copy-start.1 = (f32[512]{0:T(512)S(1)}, f32[512]{0:T(512)}, u32[]{:S(2)}) copy-start(f32[512]{0:T(512)} %param.21) | copy-start | bytes 6148
  48.3 33.0 %all-to-all-start = ((f32[4,4,8,2048]{3,1,0,2:T(4,128)}), f32[4,4,8,2048]{3,1,0,2:T(4,128)S(1)}, u32[]{:S(2)}, u32[]{:S(2)}) async-start(f32[4,4,8,2048]{3,1,0,2:T(4,128)} %bitcast.36), calls=%async_computation | async-start | bytes 2097152 | tf_op jit(solution)/shard_map/all_to_all | solution.py:65
  53.7 47.9 %all-gather.2.cloned.1.call-start = ((), (), s32[]{:S(2)}) async-start(), calls=%async_computation.2 | async-start | bytes 1179648 | tf_op jit(solution)/shard_map/all_gather | solution.py:51
  215.8 28.3 %all-to-all-start.1 = ((f32[4,4,8,2048]{3,1,0,2:T(4,128)}), f32[4,4,8,2048]{3,1,0,2:T(4,128)S(1)}, u32[]{:S(2)}, u32[]{:S(2)}) async-start(f32[4,4,8,2048]{3,1,0,2:T(4,128)} %bitcast.35), calls=%async_computation.1 | async-start | bytes 2097152 | tf_op jit(solution)/shard_map/all_to_all | solution.py:65
Sparse Core Ops, SparseCore 0:
  56.7 44.8 all-gather.1
where the time goes:
time: 330 us; the launch traced here: 327 us
  blocking collectives  72.3 us (22%)
  waiting for transfers between devices  70.2 us (21%)
  loops' own time  69.3 us (21%)
  local copies, waits for them, and re-layouts  45.2 us (14%)
  matrix products  40.3 us (12%)
  between operations  14.1 us (4%)
  starting transfers between devices  10.5 us (3%)
  other arithmetic  5.18 us (2%)
    all_gather x2, blocking collectives, body(): residual = lax.all_gather(rounded, 'scan', axis=2, tiled=True)  60.6 us
    all_to_all x2, waiting for transfers between devices, body(): lax.all_to_all(outgoing, 'scan', split_axis=2, concat_axis=2, tiled=True)  49.4 us
    another operation x2, loops' own time, add_forward(): return lax.fori_loop(first_slot, end_slot, advance, partial_value)  34.7 us
    another operation x2, loops' own time, add_backward(): return lax.fori_loop(first_slot, end_slot, advance, gradient)  34.5 us
    dot_general x16, matrix products, advance(): jnp.einsum('fij,fsj->fsi', matrix, source, preferred_element_type=jnp.flo...  20.6 us
    all_gather x1, waiting for transfers between devices, body(): measured_all = lax.all_gather(measured, 'scan', axis=2, tiled=True)  20.1 us
    dot_general x16, matrix products, advance(): jnp.einsum('fij,fsi->fsj', matrix, source, preferred_element_type=jnp.flo...  19.7 us
    psum x2, blocking collectives, body(): energy = lax.psum(jnp.sum(moved * moved, axis=(0, 1)), 'bin')  11.7 us
  transfers between devices with their start and end apart: 3, of which 3 were waited for; matrix products, arithmetic and copies ran while one was open for 0% of the time, Pallas kernels for 0%

commit v1 on v0

--- a/solution.py
+++ b/solution.py
@@ -65,7 +65,14 @@
         arrived = lax.all_to_all(outgoing, "scan", split_axis=2, concat_axis=2, tiled=True)
         totals = jnp.sum(arrived, axis=2)
         rounded = (totals - own_measured).astype(jnp.bfloat16)
-        residual = lax.all_gather(rounded, "scan", axis=2, tiled=True)
+        ring = [rounded]
+        for hop in range(7):
+            ring.append(lax.ppermute(ring[-1], "scan", [(dev, (dev + 1) % 8) for dev in range(8)]))
+        residual = jnp.roll(
+            jnp.concatenate(ring[::-1], axis=2),
+            (lax.axis_index("scan") + 1) * ring[0].shape[2],
+            axis=2,
+        )
         gradient = jnp.zeros_like(current)
         gradient = add_backward(
             gradient, tile_blocks, block_rows, block_cols, residual, 0, live_count

time: 330 us -> 351 us (1.064)
  waiting for transfers between devices: 70.2 us -> 131 us
  blocking collectives: 72.3 us -> 40.6 us
  starting transfers between devices: 10.5 us -> 6.36 us
    ppermute x0 -> x14, waiting for transfers between devices: none -> 83.6 us  [body(): lax.ppermute(ring[-1], 'scan', [(dev, (dev + 1) % 8) for dev in range(8)])]
    all_gather x2 -> x0, blocking collectives: 60.6 us -> none  [body(): residual = lax.all_gather(rounded, 'scan', axis=2, tiled=True)]
    all_to_all x0 -> x1, blocking collectives: none -> 28.9 us  [body(): lax.all_to_all(outgoing, 'scan', split_axis=2, concat_axis=2, tiled=True)]
    all_to_all x2 -> x1, waiting for transfers between devices: 49.4 us -> 26.8 us  [body(): lax.all_to_all(outgoing, 'scan', split_axis=2, concat_axis=2, tiled=True)]
    all_to_all x2 -> x1, starting transfers between devices: 10.5 us -> 5.45 us  [body(): lax.all_to_all(outgoing, 'scan', split_axis=2, concat_axis=2, tiled=True)]
  transfers between devices with their start and end apart: 3 -> 16, of which waited for: 3 -> 16; matrix products, arithmetic and copies ran while one was open for 0% -> 0% of each run, Pallas kernels for 0% -> 0%
where the time goes in v1:
time: 351 us; the launch traced here: 349 us
  waiting for transfers between devices  131 us (37%)
  loops' own time  66.2 us (19%)
  local copies, waits for them, and re-layouts  42.8 us (12%)
  blocking collectives  40.6 us (12%)
  matrix products  40.3 us (11%)
  between operations  14.2 us (4%)
  other arithmetic  6.82 us (2%)
  starting transfers between devices  6.36 us (2%)
    ppermute x14, waiting for transfers between devices, body(): lax.ppermute(ring[-1], 'scan', [(dev, (dev + 1) % 8) for dev in range(8)])  83.6 us
    another operation x2, loops' own time, add_forward(): return lax.fori_loop(first_slot, end_slot, advance, partial_value)  33.2 us
    another operation x2, loops' own time, add_backward(): return lax.fori_loop(first_slot, end_slot, advance, gradient)  33 us
    all_to_all x1, blocking collectives, body(): lax.all_to_all(outgoing, 'scan', split_axis=2, concat_axis=2, tiled=True)  28.9 us
    all_to_all x1, waiting for transfers between devices, body(): lax.all_to_all(outgoing, 'scan', split_axis=2, concat_axis=2, tiled=True)  26.8 us
    dot_general x16, matrix products, advance(): jnp.einsum('fij,fsj->fsi', matrix, source, preferred_element_type=jnp.flo...  20.6 us
    all_gather x1, waiting for transfers between devices, body(): measured_all = lax.all_gather(measured, 'scan', axis=2, tiled=True)  20.1 us
    dot_general x16, matrix products, advance(): jnp.einsum('fij,fsi->fsj', matrix, source, preferred_element_type=jnp.flo...  19.7 us
  transfers between devices with their start and end apart: 16, of which 16 were waited for; matrix products, arithmetic and copies ran while one was open for 0% of the time, Pallas kernels for 0%

profile of v1, /device:TPU:12, one launch (start us, length us, event | category | flops | bytes accessed | tf_op | source)
XLA Modules:
  0.0 348.6 jit_solution(6441512450516368854)
XLA Ops:
  8.8 38.0 %while.40 = (s32[]{:T(128)}, f32[4,4,16384]{2,1,0:T(4,128)S(1)}, s32[]{:T(128)}, s32[8]{0:T(128)S(1)}, s32[8]{0:T(128)S(1)}, /*index=5*/bf16[4,4,512]{2,1,0:T(4,...) while((s32[]{:T(128)}, f32[4,4,16384]{2,1,0:T(4,128)S(1)}, ...), condition=%wide.region_1.2_spmd, body=%wide.region_0.1_spmd.sunk | while | flops 2101261 | bytes 565535 | solution.py:20
  12.2 1.3 fusion.38
  16.9 1.3 fusion.38
  21.5 1.3 fusion.38
  26.2 1.3 fusion.38
  30.9 1.3 fusion.38
  35.5 1.3 fusion.38
  40.2 1.3 fusion.38
  44.9 1.3 fusion.38
  48.0 5.5 %all-to-all-start = ((f32[4,4,8,2048]{3,1,0,2:T(4,128)}), f32[4,4,8,2048]{3,1,0,2:T(4,128)S(1)}, u32[]{:S(2)}, u32[]{:S(2)}) async-start(f32[4,4,8,2048]{3,1,0,2:T(4,128)} %bitcast.36), calls=%async_computation | async-start | bytes 2097152 | tf_op jit(solution)/shard_map/all_to_all | solution.py:65
  54.1 26.8 %all-to-all-done = f32[4,4,8,2048]{3,1,0,2:T(4,128)S(1)} async-done(((f32[4,4,8,2048]{3,1,0,2:T(4,128)}), f32[4,4,8,2048]{3,1,0,2:T(4,128)S(1)}, u32[]{:S(2)}, u32[]{:S(2)}) %all-to-all-start) | async-done | bytes 1048608 | tf_op jit(solution)/shard_map/all_to_all | solution.py:65
  81.2 20.1 %all-gather.2.cloned.1.call-done = f32[4,4,16384]{2,1,0:T(4,128)} async-done(((f32[4,4,2048]{2,1,0:T(4,128)}), f32[4,4,16384]{2,1,0:T(4,128)}) %all-gather.2.cloned.1.call-update) | async-done | bytes 1048592 | tf_op jit(solution)/shard_map/all_gather | solution.py:51
  102.9 4.6 %collective-permute-done = bf16[4,4,2048]{2,1,0:T(4,128)(2,1)S(1)} collective-permute-done((bf16[4,4,2048]{2,1,0:T(4,128)(2,1)S(1)}, bf16[4,4,2048]{2,1,0:T(4,128)(2,1)S(1)}, u32[]{:S(2)}, u32[]{:S(2)}) %collective-permute-start) | collective-permute-done | bytes 65568 | tf_op jit(solution)/shard_map/ppermute | solution.py:70
  107.5 5.2 %collective-permute-done.1 = bf16[4,4,2048]{2,1,0:T(4,128)(2,1)S(1)} collective-permute-done((bf16[4,4,2048]{2,1,0:T(4,128)(2,1)S(1)}, bf16[4,4,2048]{2,1,0:T(4,128)(2,1)S(1)}, u32[]{:S(2)}, u32[]{:S(2)}) %collective-permute-start.1) | collective-permute-done | bytes 65568 | tf_op jit(solution)/shard_map/ppermute | solution.py:70
  112.7 5.5 %collective-permute-done.2 = bf16[4,4,2048]{2,1,0:T(4,128)(2,1)S(1)} collective-permute-done((bf16[4,4,2048]{2,1,0:T(4,128)(2,1)S(1)}, bf16[4,4,2048]{2,1,0:T(4,128)(2,1)S(1)}, u32[]{:S(2)}, u32[]{:S(2)}) %collective-permute-start.2) | collective-permute-done | bytes 65568 | tf_op jit(solution)/shard_map/ppermute | solution.py:70
  118.2 6.3 %collective-permute-done.3 = bf16[4,4,2048]{2,1,0:T(4,128)(2,1)S(1)} collective-permute-done((bf16[4,4,2048]{2,1,0:T(4,128)(2,1)S(1)}, bf16[4,4,2048]{2,1,0:T(4,128)(2,1)S(1)}, u32[]{:S(2)}, u32[]{:S(2)}) %collective-permute-start.3) | collective-permute-done | bytes 65568 | tf_op jit(solution)/shard_map/ppermute | solution.py:70
  124.5 6.9 %collective-permute-done.4 = bf16[4,4,2048]{2,1,0:T(4,128)(2,1)S(1)} collective-permute-done((bf16[4,4,2048]{2,1,0:T(4,128)(2,1)S(1)}, bf16[4,4,2048]{2,1,0:T(4,128)(2,1)S(1)}, u32[]{:S(2)}, u32[]{:S(2)}) %collective-permute-start.4) | collective-permute-done | bytes 65568 | tf_op jit(solution)/shard_map/ppermute | solution.py:70
  131.4 6.7 %collective-permute-done.5 = bf16[4,4,2048]{2,1,0:T(4,128)(2,1)S(1)} collective-permute-done((bf16[4,4,2048]{2,1,0:T(4,128)(2,1)S(1)}, bf16[4,4,2048]{2,1,0:T(4,128)(2,1)S(1)}, u32[]{:S(2)}, u32[]{:S(2)}) %collective-permute-start.5) | collective-permute-done | bytes 65568 | tf_op jit(solution)/shard_map/ppermute | solution.py:70
  138.7 6.3 %collective-permute-done.6 = bf16[4,4,2048]{2,1,0:T(4,128)(2,1)S(1)} collective-permute-done((bf16[4,4,2048]{2,1,0:T(4,128)(2,1)S(1)}, bf16[4,4,2048]{2,1,0:T(4,128)(2,1)S(1)}, u32[]{:S(2)}, u32[]{:S(2)}) %collective-permute-start.6) | collective-permute-done | bytes 65568 | tf_op jit(solution)/shard_map/ppermute | solution.py:70
  146.2 35.6 %while.41 = (s32[]{:T(128)}, f32[4,4,512]{2,1,0:T(4,128)S(1)}, s32[]{:T(128)}, s32[8]{0:T(128)S(1)}, s32[8]{0:T(128)S(1)}, /*index=5*/bf16[4,4,16384]{2,1,0:T(4,...) while((s32[]{:T(128)}, f32[4,4,512]{2,1,0:T(4,128)S(1)}, ...), condition=%wide.region_4.6_spmd, body=%wide.region_3.5_spmd.sunk | while | flops 2101261 | bytes 565535 | solution.py:34
  149.3 1.2 fusion.41
  153.7 1.2 fusion.41
  158.0 1.2 fusion.41
  162.4 1.2 fusion.41
  171.1 1.2 fusion.41
  175.5 1.2 fusion.41
  179.9 1.2 fusion.41
  181.8 5.9 %psum.14 = f32[512]{0:T(512)S(1)} all-reduce(f32[512]{0:T(512)S(1)} %get-tuple-element.218), channel_id=1, replica_groups=mesh['scan'=8,'bin'=4] {'bin'}, use_global_device_ids=true, to_apply=%region_6.8 | all-reduce | flops 512 | bytes 4096 | tf_op jit(solution)/shard_map/psum | solution.py:81
  187.9 36.1 %while.42 = (s32[]{:T(128)}, f32[4,4,16384]{2,1,0:T(4,128)S(1)}, s32[]{:T(128)}, s32[8]{0:T(128)S(1)}, s32[8]{0:T(128)S(1)}, /*index=5*/bf16[4,4,512]{2,1,0:T(4,...) while((s32[]{:T(128)}, f32[4,4,16384]{2,1,0:T(4,128)S(1)}, ...), condition=%wide.region_8.10_spmd, body=%wide.region_7.9_spmd.sunk | while | flops 2101261 | bytes 565535 | solution.py:20
  191.0 1.3 fusion.44
  195.5 1.3 fusion.44
  199.9 1.3 fusion.44
  204.3 1.3 fusion.44
  208.8 1.3 fusion.44
  213.2 1.3 fusion.44
  217.7 1.3 fusion.44
  222.1 1.3 fusion.44
  224.2 28.9 %all_to_all.10 = f32[4,4,8,2048]{3,1,0,2:T(4,128)S(1)} all-to-all(f32[4,4,8,2048]{3,1,0,2:T(4,128)S(1)} %bitcast.68), channel_id=1, replica_groups=mesh['scan'=8,'bin'=4] {'scan'}, dimensions={2} | all-to-all | bytes 2097152 | tf_op jit(solution)/shard_map/all_to_all | solution.py:65
  254.5 5.0 %collective-permute-done.7 = bf16[4,4,2048]{2,1,0:T(4,128)(2,1)S(1)} collective-permute-done((bf16[4,4,2048]{2,1,0:T(4,128)(2,1)S(1)}, bf16[4,4,2048]{2,1,0:T(4,128)(2,1)S(1)}, u32[]{:S(2)}, u32[]{:S(2)}) %collective-permute-start.7) | collective-permute-done | bytes 65568 | tf_op jit(solution)/shard_map/ppermute | solution.py:70
  259.4 5.8 %collective-permute-done.8 = bf16[4,4,2048]{2,1,0:T(4,128)(2,1)S(1)} collective-permute-done((bf16[4,4,2048]{2,1,0:T(4,128)(2,1)S(1)}, bf16[4,4,2048]{2,1,0:T(4,128)(2,1)S(1)}, u32[]{:S(2)}, u32[]{:S(2)}) %collective-permute-start.8) | collective-permute-done | bytes 65568 | tf_op jit(solution)/shard_map/ppermute | solution.py:70
  265.2 5.4 %collective-permute-done.9 = bf16[4,4,2048]{2,1,0:T(4,128)(2,1)S(1)} collective-permute-done((bf16[4,4,2048]{2,1,0:T(4,128)(2,1)S(1)}, bf16[4,4,2048]{2,1,0:T(4,128)(2,1)S(1)}, u32[]{:S(2)}, u32[]{:S(2)}) %collective-permute-start.9) | collective-permute-done | bytes 65568 | tf_op jit(solution)/shard_map/ppermute | solution.py:70
  270.6 5.8 %collective-permute-done.10 = bf16[4,4,2048]{2,1,0:T(4,128)(2,1)S(1)} collective-permute-done((bf16[4,4,2048]{2,1,0:T(4,128)(2,1)S(1)}, bf16[4,4,2048]{2,1,0:T(4,128)(2,1)S(1)}, u32[]{:S(2)}, u32[]{:S(2)}) %collective-permute-start.10) | collective-permute-done | bytes 65568 | tf_op jit(solution)/shard_map/ppermute | solution.py:70
  276.4 6.2 %collective-permute-done.11 = bf16[4,4,2048]{2,1,0:T(4,128)(2,1)S(1)} collective-permute-done((bf16[4,4,2048]{2,1,0:T(4,128)(2,1)S(1)}, bf16[4,4,2048]{2,1,0:T(4,128)(2,1)S(1)}, u32[]{:S(2)}, u32[]{:S(2)}) %collective-permute-start.11) | collective-permute-done | bytes 65568 | tf_op jit(solution)/shard_map/ppermute | solution.py:70
  282.6 7.2 %collective-permute-done.12 = bf16[4,4,2048]{2,1,0:T(4,128)(2,1)S(1)} collective-permute-done((bf16[4,4,2048]{2,1,0:T(4,128)(2,1)S(1)}, bf16[4,4,2048]{2,1,0:T(4,128)(2,1)S(1)}, u32[]{:S(2)}, u32[]{:S(2)}) %collective-permute-start.12) | collective-permute-done | bytes 65568 | tf_op jit(solution)/shard_map/ppermute | solution.py:70
  289.8 6.8 %collective-permute-done.13 = bf16[4,4,2048]{2,1,0:T(4,128)(2,1)S(1)} collective-permute-done((bf16[4,4,2048]{2,1,0:T(4,128)(2,1)S(1)}, bf16[4,4,2048]{2,1,0:T(4,128)(2,1)S(1)}, u32[]{:S(2)}, u32[]{:S(2)}) %collective-permute-start.13) | collective-permute-done | bytes 65568 | tf_op jit(solution)/shard_map/ppermute | solution.py:70
  297.8 37.5 %while.43 = (s32[]{:T(128)}, f32[4,4,512]{2,1,0:T(4,128)S(1)}, s32[]{:T(128)}, s32[8]{0:T(128)S(1)}, s32[8]{0:T(128)S(1)}, /*index=5*/bf16[4,4,16384]{2,1,0:T(4,...) while((s32[]{:T(128)}, f32[4,4,512]{2,1,0:T(4,128)S(1)}, ...), condition=%wide.region_11.13_spmd, body=%wide.region_10.12_spmd.sunk | while | flops 2101261 | bytes 565535 | solution.py:34
  301.1 1.2 fusion.47
  335.3 5.9 %psum.15 = f32[512]{0:T(512)S(1)} all-reduce(f32[512]{0:T(512)S(1)} %multiply_reduce_fusion), channel_id=1, replica_groups=mesh['scan'=8,'bin'=4] {'bin'}, use_global_device_ids=true, to_apply=%region_13.15 | all-reduce | flops 512 | bytes 4096 | tf_op jit(solution)/shard_map/psum | solution.py:81
  (129 shorter events, 61.1 us)
Async XLA Ops:
  48.0 133.8 %copy-start = (f32[4,4,512]{2,1,0:T(4,128)S(1)}, f32[4,4,512]{2,1,0:T(4,128)}, u32[]{:S(2)}) copy-start(f32[4,4,512]{2,1,0:T(4,128)} %param.20) | copy-start | bytes 98308
  48.0 139.8 %copy-start.1 = (f32[512]{0:T(512)S(1)}, f32[512]{0:T(512)}, u32[]{:S(2)}) copy-start(f32[512]{0:T(512)} %param.23) | copy-start | bytes 6148
  48.0 33.0 %all-to-all-start = ((f32[4,4,8,2048]{3,1,0,2:T(4,128)}), f32[4,4,8,2048]{3,1,0,2:T(4,128)S(1)}, u32[]{:S(2)}, u32[]{:S(2)}) async-start(f32[4,4,8,2048]{3,1,0,2:T(4,128)} %bitcast.36), calls=%async_computation | async-start | bytes 2097152 | tf_op jit(solution)/shard_map/all_to_all | solution.py:65
  53.4 47.9 %all-gather.2.cloned.1.call-start = ((), (), s32[]{:S(2)}) async-start(), calls=%async_computation.2 | async-start | bytes 1179648 | tf_op jit(solution)/shard_map/all_gather | solution.py:51
  102.3 5.2 %collective-permute-start = (bf16[4,4,2048]{2,1,0:T(4,128)(2,1)S(1)}, bf16[4,4,2048]{2,1,0:T(4,128)(2,1)S(1)}, u32[]{:S(2)}, u32[]{:S(2)}) collective-permute-start(bf16[4,4,2048]{2,1,0:T(4,128)(2,1)S(1)} %subtract_convert_fusion.1), channel_id=1, source_target_pairs={{0,4},{4,8},{8,12},{12,16},{16,20},{20,24},{24,28},{28,0},{1,5},{5... | collective-permute-start | bytes 196616 | tf_op jit(solution)/shard_map/ppermute | solution.py:70
  107.5 5.2 %collective-permute-start.1 = (bf16[4,4,2048]{2,1,0:T(4,128)(2,1)S(1)}, bf16[4,4,2048]{2,1,0:T(4,128)(2,1)S(1)}, u32[]{:S(2)}, u32[]{:S(2)}) collective-permute-start(bf16[4,4,2048]{2,1,0:T(4,128)(2,1)S(1)} %collective-permute-done), channel_id=1, source_target_pairs={{0,4},{4,8},{8,12},{12,16},{16,20},{20,24},{24,28},{28,0},{1,5},{5... | collective-permute-start | bytes 196616 | tf_op jit(solution)/shard_map/ppermute | solution.py:70
  112.7 5.5 %collective-permute-start.2 = (bf16[4,4,2048]{2,1,0:T(4,128)(2,1)S(1)}, bf16[4,4,2048]{2,1,0:T(4,128)(2,1)S(1)}, u32[]{:S(2)}, u32[]{:S(2)}) collective-permute-start(bf16[4,4,2048]{2,1,0:T(4,128)(2,1)S(1)} %collective-permute-done.1), channel_id=1, source_target_pairs={{0,4},{4,8},{8,12},{12,16},{16,20},{20,24},{24,28},{28,0},{1,5},{5... | collective-permute-start | bytes 196616 | tf_op jit(solution)/shard_map/ppermute | solution.py:70
  118.2 6.3 %collective-permute-start.3 = (bf16[4,4,2048]{2,1,0:T(4,128)(2,1)S(1)}, bf16[4,4,2048]{2,1,0:T(4,128)(2,1)S(1)}, u32[]{:S(2)}, u32[]{:S(2)}) collective-permute-start(bf16[4,4,2048]{2,1,0:T(4,128)(2,1)S(1)} %collective-permute-done.2), channel_id=1, source_target_pairs={{0,4},{4,8},{8,12},{12,16},{16,20},{20,24},{24,28},{28,0},{1,5},{5... | collective-permute-start | bytes 196616 | tf_op jit(solution)/shard_map/ppermute | solution.py:70
  124.5 6.9 %collective-permute-start.4 = (bf16[4,4,2048]{2,1,0:T(4,128)(2,1)S(1)}, bf16[4,4,2048]{2,1,0:T(4,128)(2,1)S(1)}, u32[]{:S(2)}, u32[]{:S(2)}) collective-permute-start(bf16[4,4,2048]{2,1,0:T(4,128)(2,1)S(1)} %collective-permute-done.3), channel_id=1, source_target_pairs={{0,4},{4,8},{8,12},{12,16},{16,20},{20,24},{24,28},{28,0},{1,5},{5... | collective-permute-start | bytes 196616 | tf_op jit(solution)/shard_map/ppermute | solution.py:70
  131.4 6.7 %collective-permute-start.5 = (bf16[4,4,2048]{2,1,0:T(4,128)(2,1)S(1)}, bf16[4,4,2048]{2,1,0:T(4,128)(2,1)S(1)}, u32[]{:S(2)}, u32[]{:S(2)}) collective-permute-start(bf16[4,4,2048]{2,1,0:T(4,128)(2,1)S(1)} %collective-permute-done.4), channel_id=1, source_target_pairs={{0,4},{4,8},{8,12},{12,16},{16,20},{20,24},{24,28},{28,0},{1,5},{5... | collective-permute-start | bytes 196616 | tf_op jit(solution)/shard_map/ppermute | solution.py:70
  138.1 7.0 %collective-permute-start.6 = (bf16[4,4,2048]{2,1,0:T(4,128)(2,1)S(1)}, bf16[4,4,2048]{2,1,0:T(4,128)(2,1)S(1)}, u32[]{:S(2)}, u32[]{:S(2)}) collective-permute-start(bf16[4,4,2048]{2,1,0:T(4,128)(2,1)S(1)} %collective-permute-done.5), channel_id=1, source_target_pairs={{0,4},{4,8},{8,12},{12,16},{16,20},{20,24},{24,28},{28,0},{1,5},{5... | collective-permute-start | bytes 196616 | tf_op jit(solution)/shard_map/ppermute | solution.py:70
  254.2 5.2 %collective-permute-start.7 = (bf16[4,4,2048]{2,1,0:T(4,128)(2,1)S(1)}, bf16[4,4,2048]{2,1,0:T(4,128)(2,1)S(1)}, u32[]{:S(2)}, u32[]{:S(2)}) collective-permute-start(bf16[4,4,2048]{2,1,0:T(4,128)(2,1)S(1)} %subtract_convert_fusion), channel_id=1, source_target_pairs={{0,4},{4,8},{8,12},{12,16},{16,20},{20,24},{24,28},{28,0},{1,5},{5... | collective-permute-start | bytes 196616 | tf_op jit(solution)/shard_map/ppermute | solution.py:70
  259.4 5.8 %collective-permute-start.8 = (bf16[4,4,2048]{2,1,0:T(4,128)(2,1)S(1)}, bf16[4,4,2048]{2,1,0:T(4,128)(2,1)S(1)}, u32[]{:S(2)}, u32[]{:S(2)}) collective-permute-start(bf16[4,4,2048]{2,1,0:T(4,128)(2,1)S(1)} %collective-permute-done.7), channel_id=1, source_target_pairs={{0,4},{4,8},{8,12},{12,16},{16,20},{20,24},{24,28},{28,0},{1,5},{5... | collective-permute-start | bytes 196616 | tf_op jit(solution)/shard_map/ppermute | solution.py:70
  265.2 5.4 %collective-permute-start.9 = (bf16[4,4,2048]{2,1,0:T(4,128)(2,1)S(1)}, bf16[4,4,2048]{2,1,0:T(4,128)(2,1)S(1)}, u32[]{:S(2)}, u32[]{:S(2)}) collective-permute-start(bf16[4,4,2048]{2,1,0:T(4,128)(2,1)S(1)} %collective-permute-done.8), channel_id=1, source_target_pairs={{0,4},{4,8},{8,12},{12,16},{16,20},{20,24},{24,28},{28,0},{1,5},{5... | collective-permute-start | bytes 196616 | tf_op jit(solution)/shard_map/ppermute | solution.py:70
  270.6 5.8 %collective-permute-start.10 = (bf16[4,4,2048]{2,1,0:T(4,128)(2,1)S(1)}, bf16[4,4,2048]{2,1,0:T(4,128)(2,1)S(1)}, u32[]{:S(2)}, u32[]{:S(2)}) collective-permute-start(bf16[4,4,2048]{2,1,0:T(4,128)(2,1)S(1)} %collective-permute-done.9), channel_id=1, source_target_pairs={{0,4},{4,8},{8,12},{12,16},{16,20},{20,24},{24,28},{28,0},{1,5},{5... | collective-permute-start | bytes 196616 | tf_op jit(solution)/shard_map/ppermute | solution.py:70
  276.4 6.2 %collective-permute-start.11 = (bf16[4,4,2048]{2,1,0:T(4,128)(2,1)S(1)}, bf16[4,4,2048]{2,1,0:T(4,128)(2,1)S(1)}, u32[]{:S(2)}, u32[]{:S(2)}) collective-permute-start(bf16[4,4,2048]{2,1,0:T(4,128)(2,1)S(1)} %collective-permute-done.10), channel_id=1, source_target_pairs={{0,4},{4,8},{8,12},{12,16},{16,20},{20,24},{24,28},{28,0},{1,5},{5... | collective-permute-start | bytes 196616 | tf_op jit(solution)/shard_map/ppermute | solution.py:70
  282.6 7.2 %collective-permute-start.12 = (bf16[4,4,2048]{2,1,0:T(4,128)(2,1)S(1)}, bf16[4,4,2048]{2,1,0:T(4,128)(2,1)S(1)}, u32[]{:S(2)}, u32[]{:S(2)}) collective-permute-start(bf16[4,4,2048]{2,1,0:T(4,128)(2,1)S(1)} %collective-permute-done.11), channel_id=1, source_target_pairs={{0,4},{4,8},{8,12},{12,16},{16,20},{20,24},{24,28},{28,0},{1,5},{5... | collective-permute-start | bytes 196616 | tf_op jit(solution)/shard_map/ppermute | solution.py:70
  289.8 6.8 %collective-permute-start.13 = (bf16[4,4,2048]{2,1,0:T(4,128)(2,1)S(1)}, bf16[4,4,2048]{2,1,0:T(4,128)(2,1)S(1)}, u32[]{:S(2)}, u32[]{:S(2)}) collective-permute-start(bf16[4,4,2048]{2,1,0:T(4,128)(2,1)S(1)} %collective-permute-done.12), channel_id=1, source_target_pairs={{0,4},{4,8},{8,12},{12,16},{16,20},{20,24},{24,28},{28,0},{1,5},{5... | collective-permute-start | bytes 196616 | tf_op jit(solution)/shard_map/ppermute | solution.py:70
Sparse Core Ops, SparseCore 0:
  56.4 44.8 all-gather.1
